TPU v7x, 32 devices: a whole 2x2x4 slice. The times are simulated.
32 devices in a mesh: pipe: 2 (over y), ctx: 4 (over x, core), dp: 4 (over z).
Axes of the slice: x: 2, y: 2, z: 4, core: 2. Of those that a mesh axis runs over, the one named last changes fastest.
Arguments:
- hidden_in: bfloat16 [2, 4, 2048, 3584], P('pipe', 'dp', 'ctx'), may hold values from -6 to 6
- selected: int32 [2, 4, 32, 16], P('pipe', 'dp', 'ctx'), may hold values from -1 to 31, as said below
- norm_gain: float32 [2, 3584], P('pipe'), may hold values from 0.1 to 1.9
- kv_weight: bfloat16 [2, 3584, 512], P('pipe', ('ctx', 'dp')), may hold values from -0.1875 to 0.1875
- gate_weight: bfloat16 [2, 28, 3584], P('pipe'), may hold values from -0.09375 to 0.09375
- saved_norm: bfloat16 [2, 4, 2048, 3584], P('pipe', 'dp', 'ctx'), may hold values from -6 to 6
- kv_cot: bfloat16 [2, 4, 2048, 512], P('pipe', 'dp', 'ctx'), may hold values from -0.15625 to 0.15625
- gate_cot: bfloat16 [2, 4, 2048, 28], P('pipe', 'dp', 'ctx'), may hold values from -0.15625 to 0.15625
Outputs:
- passed: bfloat16 [2, 4, 2048, 3584], P('pipe', 'dp', 'ctx')
- kv_grad: bfloat16 [2, 3584, 512], P('pipe', ('ctx', 'dp'))
- gate_grad: bfloat16 [2, 28, 3584], P('pipe', None, ('ctx', 'dp'))
Inputs may be any that keep to these rules, and one draw needn't show every extreme that they name: `selected`: for query block b, entry 0 is b; then come min(b, 15) distinct blocks below b in random order, then -1 in the remaining entries.
All inputs are finite; a program needn't handle non-finite values.
Results may differ from a plain program's by a relative error of at most 0.0061.
Values may be sent and summed in bfloat16 or wider, within the bound.
A program may use at most 128 MiB of HBM per device.

v0:
```python
import math
import jax
import jax.numpy as jnp
from jax import lax
from jax.sharding import PartitionSpec as P

H = 28
HD = 128
KVH = 2
BLOCK = 64
SEL = 16
epsilon = 1e-06


def passed_along(block, axis, distance):
    devices = range(lax.axis_size(axis))
    route = [((i - distance) % len(devices), i) for i in devices]
    return lax.ppermute(block, axis, route)


def attend_block(packed, key_rows, value_rows):
    query_block, block_picks, block_place = packed
    group = H // KVH
    chosen = jnp.maximum(block_picks, 0)
    key_tiles = jnp.take(key_rows, chosen, axis=0).reshape(SEL * BLOCK, KVH, HD)
    value_tiles = jnp.take(value_rows, chosen, axis=0).reshape(SEL * BLOCK, KVH, HD)
    query_heads = query_block.reshape(BLOCK, KVH, group, HD)
    score_scale = 1.0 / math.sqrt(HD)
    scores = (
        jnp.einsum("qgjd,kgd->gjqk", query_heads, key_tiles, preferred_element_type=jnp.float32)
        * score_scale
    )
    key_place = (chosen[:, None] * BLOCK + jnp.arange(BLOCK, dtype=jnp.int32)[None, :]).reshape(-1)
    present = jnp.broadcast_to((block_picks >= 0)[:, None], (SEL, BLOCK)).reshape(-1)
    query_place = block_place * BLOCK + jnp.arange(BLOCK, dtype=jnp.int32)
    allowed = present[None, :] & (key_place[None, :] <= query_place[:, None])
    scores = jnp.where(allowed, scores, -1e30)
    row_max = jnp.max(scores, axis=-1, keepdims=True)
    weights = jnp.exp(scores - row_max)
    denominator = jnp.sum(weights, axis=-1)
    weights_low = weights.astype(jnp.bfloat16)
    blended = jnp.einsum(
        "gjqk,kgd->qgjd", weights_low, value_tiles, preferred_element_type=jnp.float32
    )
    blended = blended / jnp.transpose(denominator, (2, 0, 1))[..., None]
    return blended.reshape(BLOCK, H * HD)


def per_device(
    hidden_in, selected, norm_gain, kv_weight, gate_weight, saved_norm, kv_cot, gate_cot
):
    current = hidden_in[0, 0]
    picks = selected[0, 0]
    length = current.shape[0]
    hidden = current.astype(jnp.float32)
    normed = (
        hidden
        * lax.rsqrt(jnp.mean(hidden * hidden, axis=-1, keepdims=True) + epsilon)
        * norm_gain[0]
    ).astype(jnp.bfloat16)
    projected = jnp.dot(
        normed,
        lax.all_gather(kv_weight[0], ("ctx", "dp"), axis=0, tiled=True),
        preferred_element_type=jnp.float32,
    ).astype(jnp.bfloat16)
    sequence_kv = lax.all_gather(projected, "ctx", axis=0, tiled=True)
    half_width = KVH * HD
    blocks_all = sequence_kv.shape[0] // BLOCK
    key_rows = sequence_kv[:, :half_width].reshape(blocks_all, BLOCK, KVH, HD)
    value_rows = sequence_kv[:, half_width:].reshape(blocks_all, BLOCK, KVH, HD)
    gating = jax.nn.sigmoid(
        lax.dot_general(
            normed, gate_weight[0], (((1,), (1,)), ((), ())), preferred_element_type=jnp.float32
        )
    )
    blocks_here = length // BLOCK
    places = lax.axis_index("ctx") * blocks_here + jnp.arange(blocks_here, dtype=jnp.int32)
    attended = lax.map(
        lambda packed: attend_block(packed, key_rows, value_rows),
        (normed.reshape(blocks_here, BLOCK, H * HD), picks, places),
    )
    attended = attended.reshape(length, H, HD)
    section_out = hidden.reshape(length, H, HD) + gating[:, :, None] * attended
    section_out = section_out.reshape(length, H * HD).astype(jnp.bfloat16)
    passed = passed_along(section_out[None, None], "pipe", 1)
    saved_rows = saved_norm[0, 0]
    local_kv = lax.dot_general(
        saved_rows, kv_cot[0, 0], (((0,), (0,)), ((), ())), preferred_element_type=jnp.float32
    )
    local_gate = lax.dot_general(
        gate_cot[0, 0], saved_rows, (((0,), (0,)), ((), ())), preferred_element_type=jnp.float32
    )
    summed_kv = lax.psum_scatter(local_kv, ("ctx", "dp"), scatter_dimension=0, tiled=True)
    summed_gate = lax.psum_scatter(local_gate, ("ctx", "dp"), scatter_dimension=1, tiled=True)
    kv_grad = summed_kv[None].astype(jnp.bfloat16)
    gate_grad = summed_gate[None].astype(jnp.bfloat16)
    return (passed, kv_grad, gate_grad)


def solution(mesh):
    in_specs = (
        P("pipe", "dp", "ctx", None),
        P("pipe", "dp", "ctx", None),
        P("pipe", None),
        P("pipe", ("ctx", "dp"), None),
        P("pipe", None, None),
        P("pipe", "dp", "ctx", None),
        P("pipe", "dp", "ctx", None),
        P("pipe", "dp", "ctx", None),
    )
    out_specs = (
        P("pipe", "dp", "ctx", None),
        P("pipe", ("ctx", "dp"), None),
        P("pipe", None, ("ctx", "dp")),
    )
    return jax.shard_map(
        per_device, mesh=mesh, in_specs=in_specs, out_specs=out_specs, check_vma=False
    )
```

profile of v0, /device:TPU:0, one launch (start us, length us, event | category | flops | bytes accessed | tf_op | source)
XLA Modules:
  0.0 360.6 jit_solution(8013587021462063414)
XLA Ops:
  8.0 5.9 %copy.34 = bf16[1,1,512,3584]{2,3,1,0:T(8,128)(2,1)} copy(bf16[1,1,512,3584]{3,2,1,0:T(8,128)(2,1)} %param.12) | data formatting | bytes 7340032 | tf_op args[0]
  13.9 2.9 fusion.18
  16.8 43.9 %all-gather.6.cloned.1.call-done = bf16[1,3584,512]{2,1,0:T(8,128)(2,1)} async-done(((bf16[1,224,512]{2,1,0:T(8,128)(2,1)}), bf16[1,3584,512]{2,1,0:T(8,128)(2,1)}) %all-gather.6.cloned.1.call-update) | async-done | bytes 3670032 | tf_op jit(solution)/shard_map/all_gather | solution.py:63
  60.7 6.2 %fusion.34 = bf16[512,512]{1,0:T(8,128)(2,1)} fusion(bf16[1,3584,512]{2,1,0:T(8,128)(2,1)} %all-gather.6.cloned.1.call-done, bf16[1,1,512,3584]{2,3,1,0:T(8,128)(2,1)} %copy.34, f32[3584]{0:T(1024)S(1)} %reduce, f32[512]{0:T(512)S(1)} %add_rsqrt_fusion), kind=kOutput, calls=%fused_computation.50 | convolution fusion | flops 1886650368 | bytes 7880704 | tf_op jit(solution)/shard_map/dot_general | solution.py:61
  67.0 4.8 %convolution_bitcast_fusion = f32[3584,28]{1,0:T(8,128)} fusion(bf16[1,1,512,3584]{3,2,1,0:T(8,128)(2,1)} %param.17, bf16[1,1,512,28]{2,3,1,0:T(8,128)(2,1)S(1)} %copy-done.4), kind=kOutput, calls=%fused_computation.38 | convolution fusion | flops 102760448 | bytes 4100096
  71.9 7.4 %fusion.27 = f32[3584,512]{1,0:T(8,128)} fusion(bf16[1,1,512,3584]{3,2,1,0:T(8,128)(2,1)} %param.17, bf16[1,1,512,512]{3,2,1,0:T(8,128)(2,1)S(1)} %copy-done), kind=kOutput, calls=%fused_computation.43 | convolution fusion | flops 1879048192 | bytes 11534336 | tf_op jit(solution)/shard_map/dot_general | solution.py:87
  79.5 6.3 %copy.35 = f32[1,1,512,3584]{3,2,1,0:T(8,128)} copy(bf16[1,1,512,3584]{2,3,1,0:T(8,128)(2,1)} %copy.34) | data formatting | bytes 11010048 | tf_op jit(solution)/shard_map/convert_element_type | solution.py:55
  85.8 4.0 %fusion.48 = f32[512,28]{0,1:T(8,128)} fusion(bf16[1,1,512,3584]{2,3,1,0:T(8,128)(2,1)} %copy.34, f32[3584]{0:T(1024)S(1)} %reduce, f32[512]{0:T(512)S(1)} %add_rsqrt_fusion, bf16[1,28,3584]{2,1,0:T(8,128)(2,1)S(1)} %copy-done.6), kind=kOutput, calls=%fused_computation.54 | convolution fusion | flops 110143488 | bytes 3944448 | tf_op jit(solution)/shard_map/dot_general | solution.py:72
  89.8 6.1 %multiply_convert_fusion = bf16[8,64,3584]{2,1,0:T(8,128)(2,1)} fusion(f32[8,64,3584]{2,1,0:T(8,128)} %bitcast.106, f32[3584]{0:T(1024)S(1)} %reduce, f32[8,64]{1,0:T(8,128)S(1)} %rsqrt.13), kind=kLoop, calls=%fused_computation.36 | loop fusion | flops 5505024 | bytes 11026432 | tf_op jit(solution)/shard_map/convert_element_type | solution.py:60
  95.8 2.7 fusion.54
  98.5 1.4 reshape.143
  99.9 1.1 reshape.144
  101.0 143.4 %while.10 = (s32[]{:T(128)}, f32[8,64,3584]{2,1,0:T(8,128)}, s32[8,16]{1,0:T(8,128)}, bf16[32,64,2,128]{3,2,1,0:T(2,128)(2,1)S(1)}, s32[8]{0:T(128)S(1)}, /*inde...) while((s32[]{:T(128)}, f32[8,64,3584]{2,1,0:T(8,128)}, ...), condition=%wide.region_4.6_spmd, body=%wide.region_1.5_spmd.sunk | while | flops 960592640 | bytes 36303624 | solution.py:78
  101.7 1.6 gather_fusion
  103.3 2.9 gather_fusion.1
  111.7 1.5 fusion.62
  113.2 1.9 fusion.63
  115.2 2.0 fusion.64
  119.7 1.6 gather_fusion
  121.3 2.8 gather_fusion.1
  129.6 1.5 fusion.62
  131.2 1.9 fusion.63
  133.1 2.0 fusion.64
  135.8 1.1 constant_dynamic-update-slice_fusion.2
  137.6 1.6 gather_fusion
  139.2 2.9 gather_fusion.1
  147.6 1.5 fusion.62
  149.1 1.9 fusion.63
  151.1 2.0 fusion.64
  155.5 1.6 gather_fusion
  157.1 2.8 gather_fusion.1
  164.0 1.1 constant_dynamic-slice_fusion.3
  165.5 1.5 fusion.62
  167.0 1.9 fusion.63
  169.0 2.0 fusion.64
  173.5 1.6 gather_fusion
  175.1 2.9 gather_fusion.1
  183.5 1.5 fusion.62
  185.0 1.9 fusion.63
  187.0 2.0 fusion.64
  191.4 1.6 gather_fusion
  193.0 2.8 gather_fusion.1
  201.4 1.5 fusion.62
  202.9 1.9 fusion.63
  204.8 2.0 fusion.64
  209.3 1.6 gather_fusion
  210.9 2.9 gather_fusion.1
  219.3 1.5 fusion.62
  220.8 1.9 fusion.63
  222.7 2.0 fusion.64
  225.5 1.1 constant_dynamic-update-slice_fusion.2
  227.3 1.6 gather_fusion
  228.9 2.8 gather_fusion.1
  237.2 1.5 fusion.62
  238.8 1.9 fusion.63
  240.7 2.0 fusion.64
  244.5 8.4 %copy.36 = f32[1,1,512,3584]{2,3,1,0:T(8,128)} copy(f32[1,1,512,3584]{3,2,1,0:T(8,128)} %bitcast.109) | data formatting | bytes 14680064 | tf_op jit(solution)/shard_map/reshape | solution.py:82
  252.9 3.9 %mul.88 = f32[512,28,128]{0,2,1:T(8,128)} broadcast(f32[512,28]{0,1:T(8,128)S(1)} %copy-done.3), dimensions={0,1} | broadcast | bytes 7397376 | tf_op jit(solution)/shard_map/mul | solution.py:83
  256.8 9.6 %add_convert_fusion = bf16[1,1,512,3584]{2,3,1,0:T(8,128)(2,1)} fusion(f32[1,1,512,3584]{2,3,1,0:T(8,128)} %bitcast.107, f32[1,1,512,3584]{2,3,1,0:T(8,128)} %copy.36, bf16[1,1,512,3584]{2,3,1,0:T(8,128)(2,1)S(1)} %copy-done.2), kind=kLoop, calls=%fused_computation.35 | loop fusion | flops 7340032 | bytes 22020096 | tf_op jit(solution)/shard_map/convert_element_type | solution.py:84
  266.4 1.5 collective-permute-start
  267.9 1.6 copy.45
  269.5 1.7 convert_bitcast_fusion
  271.2 76.9 %collective-permute-done = bf16[1,1,512,3584]{2,3,1,0:T(8,128)(2,1)} collective-permute-done((bf16[1,1,512,3584]{2,3,1,0:T(8,128)(2,1)}, bf16[1,1,512,3584]{2,3,1,0:T(8,128)(2,1)}, u32[]{:S(2)}, u32[]{:S(2)}) %collective-permute-start) | collective-permute-done | bytes 3670048 | tf_op jit(solution)/shard_map/ppermute | solution.py:18
  348.2 5.9 %copy.37 = bf16[1,1,512,3584]{3,2,1,0:T(8,128)(2,1)} copy(bf16[1,1,512,3584]{2,3,1,0:T(8,128)(2,1)} %collective-permute-done) | data formatting | bytes 7340032
  (163 shorter events, 56.3 us)
Async XLA Ops:
  7.2 64.8 %copy-start = (bf16[1,1,512,512]{3,2,1,0:T(8,128)(2,1)S(1)}, bf16[1,1,512,512]{3,2,1,0:T(8,128)(2,1)}, u32[]{:S(2)}) copy-start(bf16[1,1,512,512]{3,2,1,0:T(8,128)(2,1)} %param.18) | copy-start | bytes 1572868
  7.2 6.7 %copy-start.5 = (f32[1,3584]{1,0:T(1,128)S(1)}, f32[1,3584]{1,0:T(1,128)}, u32[]{:S(2)}) copy-start(f32[1,3584]{1,0:T(1,128)} %param.14) | copy-start | bytes 43012
  7.2 53.5 %all-gather.6.cloned.1.call-start = ((), (), s32[]{:S(2)}) async-start(), calls=%async_computation.4 | async-start | bytes 3899392 | tf_op jit(solution)/shard_map/all_gather | solution.py:63
  7.9 87.9 %all-gather.4.cloned.1.call-start = ((), (), s32[]{:S(2)}) async-start(), calls=%async_computation.2 | async-start | bytes 2621440 | tf_op jit(solution)/shard_map/all_gather | solution.py:66
  16.8 50.2 %copy-start.4 = (bf16[1,1,512,28]{2,3,1,0:T(8,128)(2,1)S(1)}, bf16[1,1,512,28]{2,3,1,0:T(8,128)(2,1)}, u32[]{:S(2)}) copy-start(bf16[1,1,512,28]{2,3,1,0:T(8,128)(2,1)} %param.19) | copy-start | bytes 86020
  67.0 200.9 %reduce-scatter.7.cloned.1.call-start = ((), (), s32[]{:S(2)}) async-start(), calls=%async_computation.5 | async-start | bytes 1949696
  71.9 197.6 %reduce-scatter.5.cloned.1.call-start = ((), (), s32[]{:S(2)}) async-start(), calls=%async_computation.3 | async-start | bytes 7798784 | tf_op jit(solution)/shard_map/reduce_scatter | solution.py:93
  79.4 6.4 %copy-start.6 = (bf16[1,28,3584]{2,1,0:T(8,128)(2,1)S(1)}, bf16[1,28,3584]{2,1,0:T(8,128)(2,1)}, u32[]{:S(2)}) copy-start(bf16[1,28,3584]{2,1,0:T(8,128)(2,1)} %param.16) | copy-start | bytes 602116
  244.5 8.4 %copy-start.3 = (f32[512,28]{0,1:T(8,128)S(1)}, f32[512,28]{0,1:T(8,128)}, u32[]{:S(2)}) copy-start(f32[512,28]{0,1:T(8,128)} %fusion.48) | copy-start | bytes 172036
  252.9 3.9 %copy-start.2 = (bf16[1,1,512,3584]{2,3,1,0:T(8,128)(2,1)S(1)}, bf16[1,1,512,3584]{2,3,1,0:T(8,128)(2,1)}, u32[]{:S(2)}) copy-start(bf16[1,1,512,3584]{2,3,1,0:T(8,128)(2,1)} %copy.34) | copy-start | bytes 11010052
  256.8 97.3 %copy-start.1 = (bf16[1,1,512,512]{3,2,1,0:T(8,128)(2,1)S(1)}, bf16[1,1,512,512]{3,2,1,0:T(8,128)(2,1)}, u32[]{:S(2)}) copy-start(bf16[1,1,512,512]{3,2,1,0:T(8,128)(2,1)} %param.18) | copy-start | bytes 1572868
  266.4 81.8 %collective-permute-start = (bf16[1,1,512,3584]{2,3,1,0:T(8,128)(2,1)}, bf16[1,1,512,3584]{2,3,1,0:T(8,128)(2,1)}, u32[]{:S(2)}, u32[]{:S(2)}) collective-permute-start(bf16[1,1,512,3584]{2,3,1,0:T(8,128)(2,1)} %add_convert_fusion), channel_id=1, source_target_pairs={{16,0},{0,16},{17,1},{1,17},{18,2},{2,18},{19,3},{3,19},{20,4},{4,... | collective-permute-start | bytes 11010056 | tf_op jit(solution)/shard_map/ppermute | solution.py:18
Sparse Core Ops, SparseCore 0:
  10.3 50.3 all-gather.5
  67.1 21.2 all-gather.3
  92.1 60.6 reduce-scatter.6
  156.7 90.6 reduce-scatter.4
where the time goes:
time: 363 us; the launch traced here: 361 us
  waiting for transfers between devices  122 us (34%)
  local copies, waits for them, and re-layouts  105 us (29%)
  other arithmetic  62.2 us (17%)
  matrix products  50.9 us (14%)
  between operations  13.8 us (4%)
  loops' own time  5.53 us (2%)
    ppermute x1, waiting for transfers between devices, passed_along(): return lax.ppermute(block, axis, route)  76.9 us
    all_gather x1, waiting for transfers between devices, per_device(): lax.all_gather(kv_weight[0], ('ctx', 'dp'), axis=0, tiled=True)  43.9 us
    gather x8, local copies, waits for them, and re-layouts, attend_block(): key_tiles = jnp.take(key_rows, chosen, axis=0).reshape(SEL * BLOCK, KVH, HD)  22.8 us
    dot_general x8, matrix products, attend_block(): jnp.einsum('gjqk,kgd->qgjd', weights_low, value_tiles, preferred_element_...  16.2 us
    reduce_sum x8, other arithmetic, attend_block(): denominator = jnp.sum(weights, axis=-1)  15.4 us
    unnamed x17, local copies, waits for them, and re-layouts  13.5 us
    dynamic_slice x16, local copies, waits for them, and re-layouts, per_device(): lax.map(lambda packed: attend_block(packed, key_rows, value_rows), (norme...  13.4 us
    gather x8, local copies, waits for them, and re-layouts, attend_block(): jnp.take(value_rows, chosen, axis=0).reshape(SEL * BLOCK, KVH, HD)  12.8 us
  transfers between devices with their start and end apart: 5, of which 2 were waited for; matrix products, arithmetic and copies ran while one was open for 57% of the time, Pallas kernels for 0%

commit v1 on v0

--- a/solution.py
+++ b/solution.py
@@ -10,6 +10,28 @@
 BLOCK = 64
 SEL = 16
 epsilon = 1e-06
+
+
+def laid_out(blocks, dim):
+    blocks = jnp.moveaxis(blocks, 0, dim)
+    lengths = blocks.shape
+    return blocks.reshape(*lengths[:dim], lengths[dim] * lengths[dim + 1], *lengths[dim + 2 :])
+
+
+def gather_around(x, axis, dim):
+    length = lax.axis_size(axis)
+    pairs = [(i, (i + 1) % length) for i in range(length)]
+    back = [(b, a) for a, b in pairs]
+    lower, upper = ([], [])
+    for step in range(length - 1):
+        if step % 2 == 0:
+            lower.append(lax.ppermute(lower[-1] if lower else x, axis, pairs))
+        else:
+            upper.append(lax.ppermute(upper[-1] if upper else x, axis, back))
+    blocks = jnp.stack([*lower[::-1], x, *upper])
+    shift = lax.axis_index(axis) - len(lower)
+    blocks = blocks[(jnp.arange(length) - shift) % length]
+    return laid_out(blocks, dim)
 
 
 def passed_along(block, axis, distance):
@@ -59,9 +81,7 @@
         * norm_gain[0]
     ).astype(jnp.bfloat16)
     projected = jnp.dot(
-        normed,
-        lax.all_gather(kv_weight[0], ("ctx", "dp"), axis=0, tiled=True),
-        preferred_element_type=jnp.float32,
+        normed, gather_around(kv_weight[0], ("ctx", "dp"), 0), preferred_element_type=jnp.float32
     ).astype(jnp.bfloat16)
     sequence_kv = lax.all_gather(projected, "ctx", axis=0, tiled=True)
     half_width = KVH * HD

time: 363 us -> 418 us (1.15)
  starting transfers between devices: 1.66 us -> 32 us
  local copies, waits for them, and re-layouts: 105 us -> 124 us
    ppermute x0 -> x15, waiting for transfers between devices: none -> 47.5 us  [the longest x8 31.6 us: gather_around(): lower.append(lax.ppermute(lower[-1] if lower else x, axis, pairs))]
    all_gather x1 -> x0, waiting for transfers between devices: 43.9 us -> none  [per_device(): lax.all_gather(kv_weight[0], ('ctx', 'dp'), axis=0, tiled=True)]
    ppermute x0 -> x15, starting transfers between devices: none -> 27 us  [the longest x7 22 us: gather_around(): upper.append(lax.ppermute(upper[-1] if upper else x, axis, back))]
    unnamed x17 -> x34, local copies, waits for them, and re-layouts: 13.5 us -> 26 us
    gather x0 -> x1, local copies, waits for them, and re-layouts: none -> 4.66 us  [gather_around(): blocks = blocks[(jnp.arange(length) - shift) % length]]
  transfers between devices with their start and end apart: 5 -> 19, of which waited for: 2 -> 13; matrix products, arithmetic and copies ran while one was open for 57% -> 54% of each run, Pallas kernels for 0% -> 0%
where the time goes in v1:
time: 418 us; the launch traced here: 416 us
  waiting for transfers between devices  126 us (30%)
  local copies, waits for them, and re-layouts  124 us (30%)
  other arithmetic  62.3 us (15%)
  matrix products  50.7 us (12%)
  starting transfers between devices  32 us (8%)
  between operations  15.6 us (4%)
  loops' own time  6.2 us (1%)
    ppermute x1, waiting for transfers between devices, passed_along(): return lax.ppermute(block, axis, route)  78 us
    ppermute x8, waiting for transfers between devices, gather_around(): lower.append(lax.ppermute(lower[-1] if lower else x, axis, pairs))  31.6 us
    unnamed x34, local copies, waits for them, and re-layouts  26 us
    gather x8, local copies, waits for them, and re-layouts, attend_block(): key_tiles = jnp.take(key_rows, chosen, axis=0).reshape(SEL * BLOCK, KVH, HD)  23 us
    ppermute x7, starting transfers between devices, gather_around(): upper.append(lax.ppermute(upper[-1] if upper else x, axis, back))  22 us
    dot_general x8, matrix products, attend_block(): jnp.einsum('gjqk,kgd->qgjd', weights_low, value_tiles, preferred_element_...  16.2 us
    ppermute x7, waiting for transfers between devices, gather_around(): upper.append(lax.ppermute(upper[-1] if upper else x, axis, back))  15.9 us
    reduce_sum x8, other arithmetic, attend_block(): denominator = jnp.sum(weights, axis=-1)  15.4 us
  transfers between devices with their start and end apart: 19, of which 13 were waited for; matrix products, arithmetic and copies ran while one was open for 54% of the time, Pallas kernels for 0%

profile of v1, /device:TPU:0, one launch (start us, length us, event | category | flops | bytes accessed | tf_op | source)
XLA Modules:
  0.0 415.9 jit_solution(5364855936315450209)
XLA Ops:
  8.1 3.1 collective-permute-start
  11.2 7.9 %collective-permute-done = bf16[224,512]{1,0:T(8,128)(2,1)S(1)} collective-permute-done((bf16[224,512]{1,0:T(8,128)(2,1)}, bf16[224,512]{1,0:T(8,128)(2,1)S(1)}, u32[]{:S(2)}, u32[]{:S(2)}) %collective-permute-start) | collective-permute-done | bytes 229408 | tf_op jit(solution)/shard_map/ppermute | solution.py:28
  19.1 4.4 %collective-permute-start.8 = (bf16[224,512]{1,0:T(8,128)(2,1)}, bf16[224,512]{1,0:T(8,128)(2,1)S(1)}, u32[]{:S(2)}, u32[]{:S(2)}) collective-permute-start(bf16[224,512]{1,0:T(8,128)(2,1)} %bitcast.124), channel_id=1, source_target_pairs={{1,0},{2,1},{3,2},{4,3},{5,4},{6,5},{7,6},{8,7},{9,8},{10,9},{11,1... | collective-permute-start | bytes 688136 | tf_op jit(solution)/shard_map/ppermute | solution.py:30
  23.5 6.0 %collective-permute-done.1 = bf16[224,512]{1,0:T(8,128)(2,1)S(1)} collective-permute-done((bf16[224,512]{1,0:T(8,128)(2,1)S(1)}, bf16[224,512]{1,0:T(8,128)(2,1)S(1)}, u32[]{:S(2)}, u32[]{:S(2)}) %collective-permute-start.1) | collective-permute-done | bytes 229408 | tf_op jit(solution)/shard_map/ppermute | solution.py:28
  29.5 2.3 collective-permute-done.8
  31.8 2.8 collective-permute-start.9
  34.6 5.5 %collective-permute-done.2 = bf16[224,512]{1,0:T(8,128)(2,1)S(1)} collective-permute-done((bf16[224,512]{1,0:T(8,128)(2,1)S(1)}, bf16[224,512]{1,0:T(8,128)(2,1)S(1)}, u32[]{:S(2)}, u32[]{:S(2)}) %collective-permute-start.2) | collective-permute-done | bytes 229408 | tf_op jit(solution)/shard_map/ppermute | solution.py:28
  40.2 4.1 collective-permute-done.9
  45.2 5.5 %collective-permute-done.3 = bf16[224,512]{1,0:T(8,128)(2,1)S(1)} collective-permute-done((bf16[224,512]{1,0:T(8,128)(2,1)S(1)}, bf16[224,512]{1,0:T(8,128)(2,1)S(1)}, u32[]{:S(2)}, u32[]{:S(2)}) %collective-permute-start.3) | collective-permute-done | bytes 229408 | tf_op jit(solution)/shard_map/ppermute | solution.py:28
  50.8 5.9 %collective-permute-done.10 = bf16[224,512]{1,0:T(8,128)(2,1)S(1)} collective-permute-done((bf16[224,512]{1,0:T(8,128)(2,1)S(1)}, bf16[224,512]{1,0:T(8,128)(2,1)S(1)}, u32[]{:S(2)}, u32[]{:S(2)}) %collective-permute-start.10) | collective-permute-done | bytes 229408 | tf_op jit(solution)/shard_map/ppermute | solution.py:30
  56.7 4.7 %collective-permute-done.4 = bf16[224,512]{1,0:T(8,128)(2,1)S(1)} collective-permute-done((bf16[224,512]{1,0:T(8,128)(2,1)S(1)}, bf16[224,512]{1,0:T(8,128)(2,1)S(1)}, u32[]{:S(2)}, u32[]{:S(2)}) %collective-permute-start.4) | collective-permute-done | bytes 229408 | tf_op jit(solution)/shard_map/ppermute | solution.py:28
  61.4 5.9 %copy.34 = bf16[1,1,512,3584]{2,3,1,0:T(8,128)(2,1)} copy(bf16[1,1,512,3584]{3,2,1,0:T(8,128)(2,1)} %param.12) | data formatting | bytes 7340032 | tf_op args[0]
  67.3 4.5 %collective-permute-start.12 = (bf16[224,512]{1,0:T(8,128)(2,1)S(1)}, bf16[224,512]{1,0:T(8,128)(2,1)S(1)}, u32[]{:S(2)}, u32[]{:S(2)}) collective-permute-start(bf16[224,512]{1,0:T(8,128)(2,1)S(1)} %collective-permute-done.11), channel_id=1, source_target_pairs={{1,0},{2,1},{3,2},{4,3},{5,4},{6,5},{7,6},{8,7},{9,8},{10,9},{11,1... | collective-permute-start | bytes 688136 | tf_op jit(solution)/shard_map/ppermute | solution.py:30
  71.8 2.9 multiply_reduce_fusion
  75.5 4.6 %collective-permute-start.13 = (bf16[224,512]{1,0:T(8,128)(2,1)S(1)}, bf16[224,512]{1,0:T(8,128)(2,1)S(1)}, u32[]{:S(2)}, u32[]{:S(2)}) collective-permute-start(bf16[224,512]{1,0:T(8,128)(2,1)S(1)} %collective-permute-done.12), channel_id=1, source_target_pairs={{1,0},{2,1},{3,2},{4,3},{5,4},{6,5},{7,6},{8,7},{9,8},{10,9},{11,1... | collective-permute-start | bytes 688136 | tf_op jit(solution)/shard_map/ppermute | solution.py:30
  80.6 1.9 collective-permute-start.7
  82.5 2.9 collective-permute-done.13
  85.4 4.7 %collective-permute-start.14 = (bf16[224,512]{1,0:T(8,128)(2,1)S(1)}, bf16[224,512]{1,0:T(8,128)(2,1)S(1)}, u32[]{:S(2)}, u32[]{:S(2)}) collective-permute-start(bf16[224,512]{1,0:T(8,128)(2,1)S(1)} %collective-permute-done.13), channel_id=1, source_target_pairs={{1,0},{2,1},{3,2},{4,3},{5,4},{6,5},{7,6},{8,7},{9,8},{10,9},{11,1... | collective-permute-start | bytes 688136 | tf_op jit(solution)/shard_map/ppermute | solution.py:30
  91.5 1.6 bitcast_dynamic-update-slice_fusion.14
  93.1 1.6 bitcast_dynamic-update-slice_fusion.13
  104.7 4.7 %gather_fusion.2 = bf16[16,224,512]{2,1,0:T(8,128)(2,1)} fusion(bf16[16,224,512]{2,1,0:T(8,128)(2,1)} %bitcast_dynamic-update-slice_fusion, s32[1024]{0:T(1024)S(1)} %pad_clamp_fusion.1), kind=kCustom, calls=%fused_computation.2 | custom fusion | bytes 7340096 | tf_op jit(solution)/shard_map/gather | solution.py:33
  109.3 6.2 %convolution_convert_fusion = bf16[512,512]{1,0:T(8,128)(2,1)} fusion(bf16[3584,512]{1,0:T(8,128)(2,1)} %bitcast.121, bf16[1,1,512,3584]{2,3,1,0:T(8,128)(2,1)} %copy.34, f32[3584]{0:T(1024)S(1)} %reduce.1, f32[512]{0:T(512)S(1)} %add_rsqrt_fusion), kind=kOutput, calls=%fused_computation.40 | convolution fusion | flops 1886650368 | bytes 7880704 | tf_op jit(solution)/shard_map/dot_general | solution.py:83
  115.6 4.9 %convolution_bitcast_fusion = f32[3584,28]{1,0:T(8,128)} fusion(bf16[1,1,512,3584]{3,2,1,0:T(8,128)(2,1)} %param.17, bf16[1,1,512,28]{2,3,1,0:T(8,128)(2,1)S(1)} %copy-done.5), kind=kOutput, calls=%fused_computation.35 | convolution fusion | flops 102760448 | bytes 4100096
  120.6 7.2 %fusion.20 = f32[3584,512]{1,0:T(8,128)} fusion(bf16[1,1,512,3584]{3,2,1,0:T(8,128)(2,1)} %param.17, bf16[1,1,512,512]{3,2,1,0:T(8,128)(2,1)S(1)} %copy-done), kind=kOutput, calls=%fused_computation.38 | convolution fusion | flops 1879048192 | bytes 11534336 | tf_op jit(solution)/shard_map/dot_general | solution.py:107
  127.9 6.4 %copy.35 = f32[1,1,512,3584]{3,2,1,0:T(8,128)} copy(bf16[1,1,512,3584]{2,3,1,0:T(8,128)(2,1)} %copy.34) | data formatting | bytes 11010048 | tf_op jit(solution)/shard_map/convert_element_type | solution.py:77
  134.3 4.0 fusion.24
  138.3 6.3 %multiply_convert_fusion = bf16[8,64,3584]{2,1,0:T(8,128)(2,1)} fusion(f32[8,64,3584]{2,1,0:T(8,128)} %bitcast.117, f32[3584]{0:T(1024)S(1)} %reduce.1, f32[8,64]{1,0:T(8,128)S(1)} %rsqrt.13), kind=kLoop, calls=%fused_computation.32 | loop fusion | flops 5505024 | bytes 11026432 | tf_op jit(solution)/shard_map/convert_element_type | solution.py:82
  144.6 2.7 fusion.32
  149.7 144.7 %while.10 = (s32[]{:T(128)}, f32[8,64,3584]{2,1,0:T(8,128)}, s32[8,16]{1,0:T(8,128)}, bf16[32,64,2,128]{3,2,1,0:T(2,128)(2,1)S(1)}, s32[8]{0:T(128)S(1)}, /*inde...) while((s32[]{:T(128)}, f32[8,64,3584]{2,1,0:T(8,128)}, ...), condition=%wide.region_4.6_spmd, body=%wide.region_1.5_spmd.sunk | while | flops 960592640 | bytes 36303624 | solution.py:98
  150.4 1.6 gather_fusion
  152.0 2.8 gather_fusion.1
  162.0 1.9 fusion.42
  164.0 2.0 fusion.43
  168.5 1.6 gather_fusion
  170.1 2.8 gather_fusion.1
  180.1 1.9 fusion.42
  182.0 2.0 fusion.43
  186.5 1.6 gather_fusion
  188.2 2.8 gather_fusion.1
  198.2 1.9 fusion.42
  200.1 2.0 fusion.43
  206.2 2.9 gather_fusion.1
  216.3 1.9 fusion.42
  218.2 2.0 fusion.43
  224.3 2.8 gather_fusion.1
  234.3 1.9 fusion.42
  236.2 2.0 fusion.43
  242.3 2.9 gather_fusion.1
  252.4 1.9 fusion.42
  254.3 2.0 fusion.43
  260.4 3.1 gather_fusion.1
  270.6 1.9 fusion.42
  272.6 2.0 fusion.43
  278.7 2.8 gather_fusion.1
  288.7 1.9 fusion.42
  290.6 2.0 fusion.43
  294.4 8.4 %copy.36 = f32[1,1,512,3584]{2,3,1,0:T(8,128)} copy(f32[1,1,512,3584]{3,2,1,0:T(8,128)} %bitcast.120) | data formatting | bytes 14680064 | tf_op jit(solution)/shard_map/reshape | solution.py:102
  302.8 4.0 mul.86
  306.8 9.5 %add_convert_fusion = bf16[1,1,512,3584]{2,3,1,0:T(8,128)(2,1)} fusion(f32[1,1,512,3584]{2,3,1,0:T(8,128)} %bitcast.118, f32[1,1,512,3584]{2,3,1,0:T(8,128)} %copy.36, bf16[1,1,512,3584]{2,3,1,0:T(8,128)(2,1)S(1)} %copy-done.2), kind=kLoop, calls=%fused_computation.31 | loop fusion | flops 7340032 | bytes 22020096 | tf_op jit(solution)/shard_map/convert_element_type | solution.py:104
  316.3 4.8 %collective-permute-start.15 = (bf16[1,1,512,3584]{2,3,1,0:T(8,128)(2,1)}, bf16[1,1,512,3584]{2,3,1,0:T(8,128)(2,1)}, u32[]{:S(2)}, u32[]{:S(2)}) collective-permute-start(bf16[1,1,512,3584]{2,3,1,0:T(8,128)(2,1)} %add_convert_fusion), channel_id=1, source_target_pairs={{16,0},{0,16},{17,1},{1,17},{18,2},{2,18},{19,3},{3,19},{20,4},{4,... | collective-permute-start | bytes 11010056 | tf_op jit(solution)/shard_map/ppermute | solution.py:40
  321.1 1.7 copy.45
  322.8 78.0 %collective-permute-done.15 = bf16[1,1,512,3584]{2,3,1,0:T(8,128)(2,1)} collective-permute-done((bf16[1,1,512,3584]{2,3,1,0:T(8,128)(2,1)}, bf16[1,1,512,3584]{2,3,1,0:T(8,128)(2,1)}, u32[]{:S(2)}, u32[]{:S(2)}) %collective-permute-start.15) | collective-permute-done | bytes 3670048 | tf_op jit(solution)/shard_map/ppermute | solution.py:40
  400.8 5.9 %copy.37 = bf16[1,1,512,3584]{3,2,1,0:T(8,128)(2,1)} copy(bf16[1,1,512,3584]{2,3,1,0:T(8,128)(2,1)} %collective-permute-done.15) | data formatting | bytes 7340032
  406.7 1.7 convert_bitcast_fusion
  (211 shorter events, 95.4 us)
Async XLA Ops:
  8.0 112.6 %copy-start = (bf16[1,1,512,512]{3,2,1,0:T(8,128)(2,1)S(1)}, bf16[1,1,512,512]{3,2,1,0:T(8,128)(2,1)}, u32[]{:S(2)}) copy-start(bf16[1,1,512,512]{3,2,1,0:T(8,128)(2,1)} %param.18) | copy-start | bytes 1572868
  8.0 136.6 %all-gather.2.cloned.1.call-start = ((), (), s32[]{:S(2)}) async-start(), calls=%async_computation.2 | async-start | bytes 2621440 | tf_op jit(solution)/shard_map/all_gather | solution.py:86
  8.1 11.0 %collective-permute-start = (bf16[224,512]{1,0:T(8,128)(2,1)}, bf16[224,512]{1,0:T(8,128)(2,1)S(1)}, u32[]{:S(2)}, u32[]{:S(2)}) collective-permute-start(bf16[224,512]{1,0:T(8,128)(2,1)} %bitcast.123), channel_id=1, source_target_pairs={{0,1},{1,2},{2,3},{3,4},{4,5},{5,6},{6,7},{7,8},{8,9},{9,10},{10,1... | collective-permute-start | bytes 688136 | tf_op jit(solution)/shard_map/ppermute | solution.py:28
  19.1 10.5 %collective-permute-start.1 = (bf16[224,512]{1,0:T(8,128)(2,1)S(1)}, bf16[224,512]{1,0:T(8,128)(2,1)S(1)}, u32[]{:S(2)}, u32[]{:S(2)}) collective-permute-start(bf16[224,512]{1,0:T(8,128)(2,1)S(1)} %collective-permute-done), channel_id=1, source_target_pairs={{0,1},{1,2},{2,3},{3,4},{4,5},{5,6},{6,7},{7,8},{8,9},{9,10},{10,1... | collective-permute-start | bytes 688136 | tf_op jit(solution)/shard_map/ppermute | solution.py:28
  19.1 12.8 %collective-permute-start.8 = (bf16[224,512]{1,0:T(8,128)(2,1)}, bf16[224,512]{1,0:T(8,128)(2,1)S(1)}, u32[]{:S(2)}, u32[]{:S(2)}) collective-permute-start(bf16[224,512]{1,0:T(8,128)(2,1)} %bitcast.124), channel_id=1, source_target_pairs={{1,0},{2,1},{3,2},{4,3},{5,4},{6,5},{7,6},{8,7},{9,8},{10,9},{11,1... | collective-permute-start | bytes 688136 | tf_op jit(solution)/shard_map/ppermute | solution.py:30
  29.5 10.6 %collective-permute-start.2 = (bf16[224,512]{1,0:T(8,128)(2,1)S(1)}, bf16[224,512]{1,0:T(8,128)(2,1)S(1)}, u32[]{:S(2)}, u32[]{:S(2)}) collective-permute-start(bf16[224,512]{1,0:T(8,128)(2,1)S(1)} %collective-permute-done.1), channel_id=1, source_target_pairs={{0,1},{1,2},{2,3},{3,4},{4,5},{5,6},{6,7},{7,8},{8,9},{9,10},{10,1... | collective-permute-start | bytes 688136 | tf_op jit(solution)/shard_map/ppermute | solution.py:28
  31.8 12.4 %collective-permute-start.9 = (bf16[224,512]{1,0:T(8,128)(2,1)S(1)}, bf16[224,512]{1,0:T(8,128)(2,1)S(1)}, u32[]{:S(2)}, u32[]{:S(2)}) collective-permute-start(bf16[224,512]{1,0:T(8,128)(2,1)S(1)} %collective-permute-done.8), channel_id=1, source_target_pairs={{1,0},{2,1},{3,2},{4,3},{5,4},{6,5},{7,6},{8,7},{9,8},{10,9},{11,1... | collective-permute-start | bytes 688136 | tf_op jit(solution)/shard_map/ppermute | solution.py:30
  40.2 10.6 %collective-permute-start.3 = (bf16[224,512]{1,0:T(8,128)(2,1)S(1)}, bf16[224,512]{1,0:T(8,128)(2,1)S(1)}, u32[]{:S(2)}, u32[]{:S(2)}) collective-permute-start(bf16[224,512]{1,0:T(8,128)(2,1)S(1)} %collective-permute-done.2), channel_id=1, source_target_pairs={{0,1},{1,2},{2,3},{3,4},{4,5},{5,6},{6,7},{7,8},{8,9},{9,10},{10,1... | collective-permute-start | bytes 688136 | tf_op jit(solution)/shard_map/ppermute | solution.py:28
  44.2 12.4 %collective-permute-start.10 = (bf16[224,512]{1,0:T(8,128)(2,1)S(1)}, bf16[224,512]{1,0:T(8,128)(2,1)S(1)}, u32[]{:S(2)}, u32[]{:S(2)}) collective-permute-start(bf16[224,512]{1,0:T(8,128)(2,1)S(1)} %collective-permute-done.9), channel_id=1, source_target_pairs={{1,0},{2,1},{3,2},{4,3},{5,4},{6,5},{7,6},{8,7},{9,8},{10,9},{11,1... | collective-permute-start | bytes 688136 | tf_op jit(solution)/shard_map/ppermute | solution.py:30
  50.8 10.6 %collective-permute-start.4 = (bf16[224,512]{1,0:T(8,128)(2,1)S(1)}, bf16[224,512]{1,0:T(8,128)(2,1)S(1)}, u32[]{:S(2)}, u32[]{:S(2)}) collective-permute-start(bf16[224,512]{1,0:T(8,128)(2,1)S(1)} %collective-permute-done.3), channel_id=1, source_target_pairs={{0,1},{1,2},{2,3},{3,4},{4,5},{5,6},{6,7},{7,8},{8,9},{9,10},{10,1... | collective-permute-start | bytes 688136 | tf_op jit(solution)/shard_map/ppermute | solution.py:28
  56.7 10.7 %collective-permute-start.11 = (bf16[224,512]{1,0:T(8,128)(2,1)S(1)}, bf16[224,512]{1,0:T(8,128)(2,1)S(1)}, u32[]{:S(2)}, u32[]{:S(2)}) collective-permute-start(bf16[224,512]{1,0:T(8,128)(2,1)S(1)} %collective-permute-done.10), channel_id=1, source_target_pairs={{1,0},{2,1},{3,2},{4,3},{5,4},{6,5},{7,6},{8,7},{9,8},{10,9},{11,1... | collective-permute-start | bytes 688136 | tf_op jit(solution)/shard_map/ppermute | solution.py:30
  61.4 10.5 %collective-permute-start.5 = (bf16[224,512]{1,0:T(8,128)(2,1)S(1)}, bf16[224,512]{1,0:T(8,128)(2,1)S(1)}, u32[]{:S(2)}, u32[]{:S(2)}) collective-permute-start(bf16[224,512]{1,0:T(8,128)(2,1)S(1)} %collective-permute-done.4), channel_id=1, source_target_pairs={{0,1},{1,2},{2,3},{3,4},{4,5},{5,6},{6,7},{7,8},{8,9},{9,10},{10,1... | collective-permute-start | bytes 688136 | tf_op jit(solution)/shard_map/ppermute | solution.py:28
  67.3 15.2 %copy-start.6 = (f32[1,3584]{1,0:T(1,128)S(1)}, f32[1,3584]{1,0:T(1,128)}, u32[]{:S(2)}) copy-start(f32[1,3584]{1,0:T(1,128)} %param.14) | copy-start | bytes 43012
  67.3 31.7 %copy-start.3 = (bf16[1,224,512]{2,1,0:T(8,128)(2,1)S(1)}, bf16[1,224,512]{2,1,0:T(8,128)(2,1)}, u32[]{:S(2)}) copy-start(bf16[1,224,512]{2,1,0:T(8,128)(2,1)} %param.15) | copy-start | bytes 688132
  67.3 8.1 %collective-permute-start.12 = (bf16[224,512]{1,0:T(8,128)(2,1)S(1)}, bf16[224,512]{1,0:T(8,128)(2,1)S(1)}, u32[]{:S(2)}, u32[]{:S(2)}) collective-permute-start(bf16[224,512]{1,0:T(8,128)(2,1)S(1)} %collective-permute-done.11), channel_id=1, source_target_pairs={{1,0},{2,1},{3,2},{4,3},{5,4},{6,5},{7,6},{8,7},{9,8},{10,9},{11,1... | collective-permute-start | bytes 688136 | tf_op jit(solution)/shard_map/ppermute | solution.py:30
  71.8 8.7 %collective-permute-start.6 = (bf16[224,512]{1,0:T(8,128)(2,1)S(1)}, bf16[224,512]{1,0:T(8,128)(2,1)}, u32[]{:S(2)}, u32[]{:S(2)}) collective-permute-start(bf16[224,512]{1,0:T(8,128)(2,1)S(1)} %collective-permute-done.5), channel_id=1, source_target_pairs={{0,1},{1,2},{2,3},{3,4},{4,5},{5,6},{6,7},{7,8},{8,9},{9,10},{10,1... | collective-permute-start | bytes 688136 | tf_op jit(solution)/shard_map/ppermute | solution.py:28
  75.5 9.9 %collective-permute-start.13 = (bf16[224,512]{1,0:T(8,128)(2,1)S(1)}, bf16[224,512]{1,0:T(8,128)(2,1)S(1)}, u32[]{:S(2)}, u32[]{:S(2)}) collective-permute-start(bf16[224,512]{1,0:T(8,128)(2,1)S(1)} %collective-permute-done.12), channel_id=1, source_target_pairs={{1,0},{2,1},{3,2},{4,3},{5,4},{6,5},{7,6},{8,7},{9,8},{10,9},{11,1... | collective-permute-start | bytes 688136 | tf_op jit(solution)/shard_map/ppermute | solution.py:30
  80.6 10.9 %collective-permute-start.7 = (bf16[224,512]{1,0:T(8,128)(2,1)}, bf16[224,512]{1,0:T(8,128)(2,1)}, u32[]{:S(2)}, u32[]{:S(2)}) collective-permute-start(bf16[224,512]{1,0:T(8,128)(2,1)} %collective-permute-done.6), channel_id=1, source_target_pairs={{0,1},{1,2},{2,3},{3,4},{4,5},{5,6},{6,7},{7,8},{8,9},{9,10},{10,1... | collective-permute-start | bytes 688136 | tf_op jit(solution)/shard_map/ppermute | solution.py:28
  85.4 18.6 %collective-permute-start.14 = (bf16[224,512]{1,0:T(8,128)(2,1)S(1)}, bf16[224,512]{1,0:T(8,128)(2,1)S(1)}, u32[]{:S(2)}, u32[]{:S(2)}) collective-permute-start(bf16[224,512]{1,0:T(8,128)(2,1)S(1)} %collective-permute-done.13), channel_id=1, source_target_pairs={{1,0},{2,1},{3,2},{4,3},{5,4},{6,5},{7,6},{8,7},{9,8},{10,9},{11,1... | collective-permute-start | bytes 688136 | tf_op jit(solution)/shard_map/ppermute | solution.py:30
  109.3 6.3 %copy-start.5 = (bf16[1,1,512,28]{2,3,1,0:T(8,128)(2,1)S(1)}, bf16[1,1,512,28]{2,3,1,0:T(8,128)(2,1)}, u32[]{:S(2)}) copy-start(bf16[1,1,512,28]{2,3,1,0:T(8,128)(2,1)} %param.19) | copy-start | bytes 86020
  115.6 205.5 %reduce-scatter.7.cloned.1.call-start = ((), (), s32[]{:S(2)}) async-start(), calls=%async_computation.4 | async-start | bytes 1949696
  120.5 286.2 %reduce-scatter.5.cloned.1.call-start = ((), (), s32[]{:S(2)}) async-start(), calls=%async_computation.3 | async-start | bytes 7798784 | tf_op jit(solution)/shard_map/reduce_scatter | solution.py:113
  127.9 6.4 %copy-start.7 = (bf16[1,28,3584]{2,1,0:T(8,128)(2,1)S(1)}, bf16[1,28,3584]{2,1,0:T(8,128)(2,1)}, u32[]{:S(2)}) copy-start(bf16[1,28,3584]{2,1,0:T(8,128)(2,1)} %param.16) | copy-start | bytes 602116
  294.4 8.4 %copy-start.4 = (f32[512,28]{0,1:T(8,128)S(1)}, f32[512,28]{0,1:T(8,128)}, u32[]{:S(2)}) copy-start(f32[512,28]{0,1:T(8,128)} %fusion.24) | copy-start | bytes 172036
  302.8 4.0 copy-start.2
  316.3 84.5 %collective-permute-start.15 = (bf16[1,1,512,3584]{2,3,1,0:T(8,128)(2,1)}, bf16[1,1,512,3584]{2,3,1,0:T(8,128)(2,1)}, u32[]{:S(2)}, u32[]{:S(2)}) collective-permute-start(bf16[1,1,512,3584]{2,3,1,0:T(8,128)(2,1)} %add_convert_fusion), channel_id=1, source_target_pairs={{16,0},{0,16},{17,1},{1,17},{18,2},{2,18},{19,3},{3,19},{20,4},{4,... | collective-permute-start | bytes 11010056 | tf_op jit(solution)/shard_map/ppermute | solution.py:40
  321.1 87.3 %copy-start.1 = (bf16[1,1,512,512]{3,2,1,0:T(8,128)(2,1)S(1)}, bf16[1,1,512,512]{3,2,1,0:T(8,128)(2,1)}, u32[]{:S(2)}) copy-start(bf16[1,1,512,512]{3,2,1,0:T(8,128)(2,1)} %param.18) | copy-start | bytes 1572868
Sparse Core Ops, SparseCore 0:
  115.7 26.2 all-gather.1
Sparse Core Ops, SparseCore 1:
  120.6 64.5 reduce-scatter.6
  189.0 90.3 reduce-scatter.4
